TPU v7x, 256 devices: a whole 4x4x8 slice. The times are simulated.
256 devices in a mesh: grp: 32 (over x, y, core), tp: 8 (over z).
Axes of the slice: x: 4, y: 4, z: 8, core: 2. Of those that a mesh axis runs over, the one named last changes fastest.
Arguments:
- hidden_in: bfloat16 [512, 2048], P('grp'), may hold values from -6 to 6
- norm_gain: bfloat16 [2048], replicated, may hold values from 0.099609375 to 1.8984375
- w_query: bfloat16 [2048, 2048], P(None, 'tp'), may hold values from -0.125 to 0.125
- w_keyval: bfloat16 [2048, 512], P(None, 'tp'), may hold values from -0.125 to 0.125
- w_output: bfloat16 [2048, 2048], P('tp'), may hold values from -0.125 to 0.125
- prefix_cache: bfloat16 [64, 512, 512], P('grp', 'tp'), may hold values from -130 to 130
- private_cache: bfloat16 [512, 512, 512], P('grp', 'tp'), may hold values from -130 to 130
- node_parent: int32 [64], replicated, may hold values from 0 to 3, as said below
- node_length: int32 [64], replicated, may hold values from 1 to 512, as said below
- request_node: int32 [512], replicated, may hold values from 4 to 63, as said below
- private_length: int32 [512], P('grp'), may hold values from 0 to 512, as said below
Outputs:
- hidden_out: bfloat16 [512, 2048], P('grp', 'tp')
- new_keyval: bfloat16 [512, 512], P('grp', 'tp')
Inputs may be any that keep to these rules, and one draw needn't show every extreme that they name: `node_parent`: nodes 0 to 3 are the tenants' roots and are their own parents; every other node's parent is a root, and every root has a child. `request_node`: request r belongs to tenant r // 128; its node is a non-root node whose parent is that tenant's root. `node_length`: the longest node has exactly 512 used slots. `private_length`: some request has exactly 512 used slots.
All inputs are finite; a program needn't handle non-finite values.
Results may differ from a plain program's by a relative error of at most 0.023.
Values may be sent and summed in bfloat16 or wider, within the bound.
A program may use at most 128 MiB of HBM per device.

v0:
```python
import math
import jax
import jax.numpy as jnp
from jax import lax
from jax.sharding import PartitionSpec as P

HEADS = 32
KV_HEADS = 4
HEAD_DIM = 64
TENANTS = 4


def combined_all(x, axis, combine):
    everything = jax.tree.map(
        lambda part, kind: lax.all_gather(part.astype(kind), axis),
        x,
        (jnp.bfloat16, jnp.bfloat16, jnp.bfloat16),
    )

    def take(k):
        return jax.tree.map(lambda part, own: part[k].astype(own.dtype), everything, x)

    return lax.fori_loop(
        1, lax.axis_size(axis), lambda k, so_far: combine(so_far, take(k)), take(0)
    )


def rms_norm(values, scale_gain):
    floats = values.astype(jnp.float32)
    spread = jnp.mean(floats * floats, axis=-1, keepdims=True)
    return (floats * lax.rsqrt(spread + 1e-05) * scale_gain.astype(jnp.float32)).astype(
        jnp.bfloat16
    )


def rotate(head_rows, position):
    half_dim = head_rows.shape[-1] // 2
    freq_index = jnp.arange(half_dim, dtype=jnp.float32)
    frequency = jnp.exp(freq_index * (-2.0 * math.log(10000.0) / head_rows.shape[-1]))
    angles = position[:, None, None] * frequency[None, None, :]
    cosine = jnp.cos(angles)
    sine_part = jnp.sin(angles)
    front_half = head_rows[..., :half_dim]
    back_half = head_rows[..., half_dim:]
    return jnp.concatenate(
        [front_half * cosine - back_half * sine_part, back_half * cosine + front_half * sine_part],
        axis=-1,
    )


def softmax_part(queries, key_rows, value_rows, valid, shared):
    row_count = queries.shape[0]
    grouped = queries.reshape(row_count, KV_HEADS, HEADS // KV_HEADS, HEAD_DIM)
    if shared:
        scores = jnp.einsum("nkgd,lkd->nkgl", grouped, key_rows, preferred_element_type=jnp.float32)
    else:
        scores = jnp.einsum(
            "nkgd,nlkd->nkgl", grouped, key_rows, preferred_element_type=jnp.float32
        )
    scores = scores * HEAD_DIM ** (-0.5)
    usable = valid[:, None, None, :]
    scores = jnp.where(usable, scores, -jnp.inf)
    maxima = jnp.maximum(jnp.max(scores, axis=-1), -1e30)
    weights = jnp.where(usable, jnp.exp(scores - maxima[..., None]), 0.0)
    totals = jnp.sum(weights, axis=-1)
    rounded = weights.astype(jnp.bfloat16)
    if shared:
        weighted = jnp.einsum(
            "nkgl,lkd->nkgd", rounded, value_rows, preferred_element_type=jnp.float32
        )
    else:
        weighted = jnp.einsum(
            "nkgl,nlkd->nkgd", rounded, value_rows, preferred_element_type=jnp.float32
        )
    return (weighted, maxima, totals)


def merge_pair(left_part, right_part):
    left_sum, left_max, left_total = left_part
    right_sum, right_max, right_total = right_part
    upper = jnp.maximum(left_max, right_max)
    left_factor = jnp.exp(left_max - upper)
    right_factor = jnp.exp(right_max - upper)
    merged_sum = left_sum * left_factor[..., None] + right_sum * right_factor[..., None]
    return (merged_sum, upper, left_total * left_factor + right_total * right_factor)


def add_token(weighted, maxima, totals, token_score, token_value, form):
    upper = jnp.maximum(maxima, token_score)
    former = jnp.exp(maxima - upper)
    fresh = jnp.exp(token_score - upper)
    summed = weighted * former[..., None] + jnp.einsum(
        form, fresh.astype(jnp.bfloat16), token_value, preferred_element_type=jnp.float32
    )
    return summed / (totals * former + fresh)[..., None]


def on_device(
    hidden_in,
    norm_gain,
    w_query,
    w_keyval,
    w_output,
    prefix_cache,
    private_cache,
    node_parent,
    node_length,
    request_node,
    private_length,
):
    grp_index = lax.axis_index("grp")
    tp_index = lax.axis_index("tp")
    req_dev = hidden_in.shape[0]
    total_req = request_node.shape[0]
    per_tenant = total_req // TENANTS
    share_count = HEADS // KV_HEADS
    key_width = KV_HEADS * HEAD_DIM
    local_heads = w_query.shape[1] // HEAD_DIM
    local_kv = w_keyval.shape[1] // HEAD_DIM
    slice_width = local_heads * HEAD_DIM
    node_dev = prefix_cache.shape[0]
    local_len = prefix_cache.shape[1]
    priv_len = private_cache.shape[1]
    scale_factor = HEAD_DIM ** (-0.5)
    normed = rms_norm(hidden_in, norm_gain)
    query = jnp.dot(normed, w_query, preferred_element_type=jnp.float32)
    keyval = jnp.dot(normed, w_keyval, preferred_element_type=jnp.float32)
    own_mid = lax.dynamic_slice_in_dim(request_node, grp_index * req_dev, req_dev)
    own_root = node_parent[own_mid]
    position = (node_length[own_root] + node_length[own_mid] + private_length).astype(jnp.float32)
    query_rot = (
        rotate(query.reshape(req_dev, local_heads, HEAD_DIM), position)
        .reshape(req_dev, slice_width)
        .astype(jnp.bfloat16)
    )
    kv_rows = keyval.reshape(req_dev, local_kv, HEAD_DIM)
    is_key = tp_index * local_kv + jnp.arange(local_kv) < KV_HEADS
    new_keyval = (
        jnp.where(is_key[None, :, None], rotate(kv_rows, position), kv_rows)
        .reshape(req_dev, local_kv * HEAD_DIM)
        .astype(jnp.bfloat16)
    )
    query_all, keyval_all = (
        lax.all_gather(query_rot, "tp", axis=1, tiled=True),
        lax.all_gather(new_keyval, "tp", axis=1, tiled=True),
    )
    everyone = lax.all_gather(query_all, "grp", axis=0, tiled=True)
    private_valid = (tp_index * priv_len + jnp.arange(priv_len))[None, :] < private_length[:, None]
    private_keys = private_cache[:, :, :key_width].reshape(req_dev, priv_len, KV_HEADS, HEAD_DIM)
    private_values = private_cache[:, :, key_width:].reshape(req_dev, priv_len, KV_HEADS, HEAD_DIM)
    private_part = softmax_part(query_all, private_keys, private_values, private_valid, False)
    slot_positions = tp_index * local_len + jnp.arange(local_len)
    node_parts = []
    for node_slot in range(node_dev):
        node_id = grp_index * node_dev + node_slot
        is_root = node_id < TENANTS
        member = jnp.where(is_root, node_parent[request_node] == node_id, request_node == node_id)
        order_key = jnp.where(member, 0, total_req) + jnp.arange(total_req)
        picked = lax.top_k(-order_key, per_tenant)[1]
        filled = jnp.arange(per_tenant) < jnp.sum(member.astype(jnp.int32))
        chosen = jnp.take(everyone, picked, axis=0)
        node_rows = prefix_cache[node_slot]
        node_keys = node_rows[:, :key_width].reshape(local_len, KV_HEADS, HEAD_DIM)
        node_values = node_rows[:, key_width:].reshape(local_len, KV_HEADS, HEAD_DIM)
        node_valid = (slot_positions < node_length[node_id])[None, :]
        weighted, maxima, totals = softmax_part(chosen, node_keys, node_values, node_valid, True)
        level_slot = jnp.where(is_root, 0, 1)
        node_parts.append((picked, filled, level_slot, weighted, maxima, totals))
    sum_rows = jnp.zeros((total_req, 2, HEADS * HEAD_DIM), jnp.float32)
    max_rows = jnp.zeros((total_req, 2, HEADS), jnp.float32)
    total_rows = jnp.zeros((total_req, 2, HEADS), jnp.float32)
    for entry in node_parts:
        picked, filled, level_slot, weighted, maxima, totals = entry
        keep = filled[:, None]
        sum_rows = sum_rows.at[picked, level_slot].add(
            jnp.where(keep, weighted.reshape(per_tenant, HEADS * HEAD_DIM), 0.0)
        )
        max_rows = max_rows.at[picked, level_slot].add(
            jnp.where(keep, maxima.reshape(per_tenant, HEADS), 0.0)
        )
        total_rows = total_rows.at[picked, level_slot].add(
            jnp.where(keep, totals.reshape(per_tenant, HEADS), 0.0)
        )
    back_sum, back_max, back_total = (
        lax.psum_scatter(sum_rows, "grp", scatter_dimension=0, tiled=True),
        lax.psum_scatter(max_rows, "grp", scatter_dimension=0, tiled=True),
        lax.psum_scatter(total_rows, "grp", scatter_dimension=0, tiled=True),
    )
    stat_shape = (req_dev, 2, KV_HEADS, share_count)
    back_sum = back_sum.reshape(req_dev, 2, KV_HEADS, share_count, HEAD_DIM)
    back_max = back_max.reshape(stat_shape)
    back_total = back_total.reshape(stat_shape)
    root_part = (back_sum[:, 0], back_max[:, 0], back_total[:, 0])
    mid_part = (back_sum[:, 1], back_max[:, 1], back_total[:, 1])
    local_sum, local_max, local_total = merge_pair(merge_pair(root_part, mid_part), private_part)
    full_sum, full_max, full_total = combined_all(
        (local_sum, local_max, local_total), "tp", merge_pair
    )
    grouped = query_all.reshape(req_dev, KV_HEADS, share_count, HEAD_DIM)
    token_keys = keyval_all[:, :key_width].reshape(req_dev, KV_HEADS, HEAD_DIM)
    token_values = keyval_all[:, key_width:].reshape(req_dev, KV_HEADS, HEAD_DIM)
    token_score = (
        jnp.einsum("nkgd,nkd->nkg", grouped, token_keys, preferred_element_type=jnp.float32)
        * scale_factor
    )
    attention_all = (
        add_token(full_sum, full_max, full_total, token_score, token_values, "nkg,nkd->nkgd")
        .reshape(req_dev, HEADS * HEAD_DIM)
        .astype(jnp.bfloat16)
    )
    attention = lax.dynamic_slice_in_dim(attention_all, tp_index * slice_width, slice_width, 1)
    projected = jnp.dot(attention, w_output, preferred_element_type=jnp.float32)
    summed = lax.psum_scatter(
        projected.astype(jnp.bfloat16), "tp", scatter_dimension=1, tiled=True
    ).astype(jnp.float32)
    out_width = summed.shape[1]
    residual = lax.dynamic_slice_in_dim(hidden_in, tp_index * out_width, out_width, 1).astype(
        jnp.float32
    )
    hidden_out = (summed + residual).astype(jnp.bfloat16)
    return (hidden_out, new_keyval)


def solution(mesh):
    placed = (
        P("grp", None),
        P(),
        P(None, "tp"),
        P(None, "tp"),
        P("tp", None),
        P("grp", "tp", None),
        P("grp", "tp", None),
        P(),
        P(),
        P(),
        P("grp"),
    )
    return jax.shard_map(
        on_device,
        mesh=mesh,
        in_specs=placed,
        out_specs=(P("grp", "tp"), P("grp", "tp")),
        check_vma=False,
    )
```

profile of v0, /device:TPU:10, one launch (start us, length us, event | category | flops | bytes accessed | tf_op | source)
XLA Modules:
  0.0 476.1 jit_solution(16032584762213668495)
XLA Ops:
  7.3 0.8 compare_select_fusion.3
  8.1 1.3 gather_fusion
  9.4 1.3 gather_fusion.2
  10.7 1.3 gather_fusion.1
  12.1 0.7 convert_element_type.137
  12.8 1.0 fusion.32
  13.8 1.6 fusion.59
  15.4 0.7 add_convert_fusion.2
  16.5 30.2 %all_gather.23 = bf16[16,2048]{1,0:T(8,128)(2,1)} all-gather(bf16[16,256]{1,0:T(8,128)(2,1)S(1)} %convert_element_type.140), channel_id=1, replica_groups=mesh['grp'=32,'tp'=8] {'tp'}, dimensions={1}, use_global_device_ids=true | all-gather | bytes 73728 | tf_op jit(solution)/shard_map/all_gather | solution.py:144
  46.7 0.9 slice_bitcast_fusion.2
  48.1 1.6 fusion.90
  49.7 2.1 fusion.87
  51.8 2.1 fusion.88
  53.8 2.1 fusion.89
  55.9 41.3 %convert_reduce_fusion = (s32[]{:T(128)}, pred[512]{0:T(512)(128)(4,1)S(1)}, s32[512]{0:T(512)S(1)}) fusion(s32[512]{0:T(512)} %param.24, s32[]{:T(128)S(6)} %add.231, pred[]{:T(512)S(6)} %lt.150, s32[]{:T(128)} %bitcast.67, s32[]{:T(128)} %bitcast.66, s32[]{:T(128)} %bitcast.65, s32[]{:T(128)} %bitcast.64, s32[]{:T(128)} %bitcast.63, s32[]{:T(128)} %bitcast.62, ...), kind=kLoop, calls=%fused_computation.153 | loop fusion | flops 68607 | bytes 4873 | tf_op jit(solution)/shard_map/reduce_sum | solution.py:160
  97.2 1.3 convert_reduce_fusion.1
  98.6 3.8 top_k.17
  102.3 3.8 top_k.24
  106.1 1.3 fusion.86
  107.5 0.6 iota_compare_fusion.1
  108.1 0.6 iota_compare_fusion
  108.8 1.3 broadcast_compare_fusion.1
  110.2 4.3 gather_fusion.3
  114.5 2.0 broadcast_select_fusion.3
  116.4 2.0 copy.74
  118.5 1.3 fusion.91
  119.9 0.9 copy-done.2
  121.2 1.7 gather_fusion.4
  122.9 1.2 broadcast_select_fusion.2
  124.3 0.3 fusion.92
  125.0 0.3 copy-done.9
  125.6 1.6 fusion.18
  127.2 1.3 copy.77
  128.5 1.4 broadcast_select_fusion.1
  129.9 2.1 fusion.16
  132.0 1.6 copy.81
  133.5 1.1 broadcast_select_fusion
  134.8 6.8 %scatter_fusion.4 = f32[512,2,32]{2,1,0:T(2,128)S(1)} fusion(f32[512,2,32]{2,1,0:T(2,128)S(1)} %broadcast.255.clone.1, s32[128]{0:T(128)S(1)} %fusion.77, f32[128,32]{1,0:T(8,128)S(1)} %copy.94), kind=kCustom, calls=%fused_computation.9 | custom fusion | flops 4096 | bytes 50176 | tf_op jit(solution)/shard_map/scatter-add | solution.py:181
  141.7 6.6 %scatter_fusion.2 = f32[512,2,32]{2,1,0:T(2,128)S(1)} fusion(f32[512,2,32]{2,1,0:T(2,128)S(1)} %broadcast.255.clone, s32[128]{0:T(128)S(1)} %fusion.77, f32[128,32]{1,0:T(8,128)S(1)} %copy.83), kind=kCustom, calls=%fused_computation.7 | custom fusion | flops 4096 | bytes 50176 | tf_op jit(solution)/shard_map/scatter-add | solution.py:178
  148.3 6.6 %scatter_fusion.5 = f32[512,2,32]{2,1,0:T(2,128)S(1)} fusion(f32[512,2,32]{2,1,0:T(2,128)S(1)} %scatter_fusion.4, s32[128]{0:T(128)S(1)} %fusion.78, f32[128,32]{1,0:T(8,128)S(1)} %copy.95), kind=kCustom, calls=%fused_computation.10 | custom fusion | flops 4096 | bytes 50176 | tf_op jit(solution)/shard_map/scatter-add | solution.py:181
  154.9 6.6 %scatter_fusion.3 = f32[512,2,32]{2,1,0:T(2,128)S(1)} fusion(f32[512,2,32]{2,1,0:T(2,128)S(1)} %scatter_fusion.2, s32[128]{0:T(128)S(1)} %fusion.78, f32[128,32]{1,0:T(8,128)S(1)} %copy.84), kind=kCustom, calls=%fused_computation.8 | custom fusion | flops 4096 | bytes 50176 | tf_op jit(solution)/shard_map/scatter-add | solution.py:178
  161.5 7.5 %broadcast_in_dim.180 = f32[512,2,2048]{2,1,0:T(2,128)} broadcast(f32[]{:T(128)} %constant.85.clone.1), dimensions={} | broadcast | bytes 8388612 | tf_op jit(solution)/shard_map/broadcast_in_dim | solution.py:169
  169.0 21.2 %scatter_fusion = f32[512,2,2048]{2,1,0:T(2,128)} fusion(f32[512,2,2048]{2,1,0:T(2,128)} %broadcast_in_dim.180, s32[128]{0:T(128)S(1)} %fusion.77, f32[128,2048]{1,0:T(8,128)S(1)} %broadcast_select_fusion.1), kind=kCustom, calls=%fused_computation.5 | custom fusion | flops 262144 | bytes 3146752 | tf_op jit(solution)/shard_map/scatter-add | solution.py:175
  190.3 22.7 %scatter_fusion.1 = f32[512,2,2048]{2,1,0:T(2,128)} fusion(f32[512,2,2048]{2,1,0:T(2,128)} %scatter_fusion, s32[128]{0:T(128)S(1)} %fusion.78, f32[128,2048]{1,0:T(8,128)} %broadcast_select_fusion), kind=kCustom, calls=%fused_computation.6 | custom fusion | flops 262144 | bytes 3146752 | tf_op jit(solution)/shard_map/scatter-add | solution.py:175
  213.1 0.7 copy-done.6
  214.4 0.4 reshape.467
  214.9 0.7 fusion.93
  215.7 1.4 reshape.468
  217.1 1.2 fusion.57
  218.5 24.5 %all-gather.1 = bf16[8,64,16]{1,2,0:T(8,128)(2,1)S(1)} all-gather(bf16[1,64,16]{1,2,0:T(8,128)(2,1)S(1)} %bitcast.283), channel_id=1, replica_groups=mesh['grp'=32,'tp'=8] {'tp'}, dimensions={0}, use_global_device_ids=true | all-gather | bytes 18432 | tf_op jit(solution)/shard_map/all_gather | solution.py:145
  243.3 0.6 dynamic-slice
  244.7 99.7 %all-reduce.8.cloned.1.call-done = (f32[512,2,2048]{2,1,0:T(2,128)}, f32[512,2,32]{2,1,0:T(2,128)}, f32[512,2,32]{2,1,0:T(2,128)}) async-done(((f32[512,2,2048]{2,1,0:T(2,128)}, f32[512,2,32]{2,1,0:T(2,128)}, f32[512,2,32]{2,1,0:T(2,128)}), (f32[512,2,2048]{2,1,0:T(2,128)}, f32[512,2,32]{2,1,0:T(2,128)}, f32[512,2,32]{2,1,0:T(2,128)})) %all-reduce.8.cloned.1.call-update) | async-done | bytes 8650768
  344.4 0.7 constant_dynamic-slice_fusion.3
  345.4 0.3 fusion.30
  345.7 0.7 constant_dynamic-slice_fusion.2
  346.6 26.0 %all_gather.28 = bf16[8,16,4,8]{1,3,2,0:T(8,128)(2,1)S(1)} all-gather(bf16[1,16,4,8]{1,3,2,0:T(8,128)(2,1)S(1)} %fusion.49), channel_id=1, replica_groups=mesh['grp'=32,'tp'=8] {'tp'}, dimensions={0}, use_global_device_ids=true | all-gather | bytes 9216 | tf_op jit(solution)/shard_map/all_gather | solution.py:15
  372.9 1.0 constant_dynamic-slice_fusion.4
  374.4 1.7 fusion.9
  376.1 26.8 %all-gather = bf16[128,4,8,64]{3,2,1,0:T(8,128)(2,1)S(1)} all-gather(bf16[16,4,8,64]{3,2,1,0:T(8,128)(2,1)S(1)} %fusion.9), channel_id=2, replica_groups=mesh['grp'=32,'tp'=8] {'tp'}, dimensions={0}, use_global_device_ids=true | all-gather | bytes 589824 | tf_op jit(solution)/shard_map/all_gather | solution.py:15
  402.9 24.6 %all_gather.27 = bf16[8,16,4,8]{1,3,2,0:T(8,128)(2,1)S(1)} all-gather(bf16[1,16,4,8]{1,3,2,0:T(8,128)(2,1)S(1)} %fusion.56), channel_id=1, replica_groups=mesh['grp'=32,'tp'=8] {'tp'}, dimensions={0}, use_global_device_ids=true | all-gather | bytes 9216 | tf_op jit(solution)/shard_map/all_gather | solution.py:15
  427.5 3.9 while.19
  431.9 0.9 convolution_convert_fusion
  432.9 35.4 %reduce-scatter.2.cloned.1.call-done = bf16[16,256]{1,0:T(8,128)(2,1)} async-done(((bf16[16,2048]{1,0:T(8,128)(2,1)}), bf16[16,256]{1,0:T(8,128)(2,1)}) %reduce-scatter.2.cloned.1.call-update) | async-done | bytes 8208 | tf_op jit(solution)/shard_map/reduce_scatter | solution.py:213
  468.2 1.3 add_convert_fusion.1
  (159 shorter events, 9.6 us)
Async XLA Ops:
  7.2 424.8 %copy-start = (bf16[256,2048]{1,0:T(8,128)(2,1)S(1)}, bf16[256,2048]{1,0:T(8,128)(2,1)}, u32[]{:S(2)}) copy-start(bf16[256,2048]{1,0:T(8,128)(2,1)} %param.19) | copy-start | bytes 3145732
  7.2 103.0 %all-gather.4.cloned.1.call-start = ((), (), s32[]{:S(2)}) async-start(), calls=%async_computation.1 | async-start | bytes 2162688 | tf_op jit(solution)/shard_map/all_gather | solution.py:147
  7.2 102.9 %copy-start.18 = (f32[32]{0:T(128)}, f32[32]{0:T(128)S(1)}, u32[]{:S(2)}) copy-start(f32[32]{0:T(128)S(1)} %multiply_exponential_fusion) | copy-start | bytes 388
  13.7 1.6 copy-start.21
  16.1 94.1 %copy-start.13 = (f32[16]{0:T(128)}, f32[16]{0:T(128)S(1)}, u32[]{:S(2)}) copy-start(f32[16]{0:T(128)S(1)} %add_convert_fusion.2) | copy-start | bytes 196
  46.7 297.8 %all-reduce.8.cloned.1.call-start = ((), (), s32[]{:S(2)}) async-start(), calls=%async_computation.3 | async-start | bytes 18874368
  108.1 16.5 %copy-start.17 = (pred[128]{0:T(512)(128)(4,1)}, pred[128]{0:T(512)(128)(4,1)S(1)}, u32[]{:S(2)}) copy-start(pred[128]{0:T(512)(128)(4,1)S(1)} %iota_compare_fusion.1) | copy-start | bytes 388
  108.8 16.2 %copy-start.15 = (pred[128]{0:T(512)(128)(4,1)}, pred[128]{0:T(512)(128)(4,1)S(1)}, u32[]{:S(2)}) copy-start(pred[128]{0:T(512)(128)(4,1)S(1)} %iota_compare_fusion) | copy-start | bytes 388
  110.0 9.8 %copy-start.12 = (pred[64]{0:T(512)(128)(4,1)}, pred[64]{0:T(512)(128)(4,1)S(1)}, u32[]{:S(2)}) copy-start(pred[64]{0:T(512)(128)(4,1)S(1)} %get-tuple-element.351) | copy-start | bytes 196
  110.0 14.6 %copy-start.11 = (pred[64]{0:T(512)(128)(4,1)}, pred[64]{0:T(512)(128)(4,1)S(1)}, u32[]{:S(2)}) copy-start(pred[64]{0:T(512)(128)(4,1)S(1)} %get-tuple-element.350) | copy-start | bytes 196
  110.2 11.0 %copy-start.1 = (bf16[512,2048]{1,0:T(8,128)(2,1)S(1)}, bf16[512,2048]{1,0:T(8,128)(2,1)}, u32[]{:S(2)}) copy-start(bf16[512,2048]{1,0:T(8,128)(2,1)} %all-gather.4.cloned.1.call-done) | copy-start | bytes 6291460
  119.8 1.0 copy-start.2
  119.8 1.2 copy-start.8
  124.7 0.6 copy-start.9
  127.2 6.3 %copy-start.16 = (pred[128]{0:T(512)(128)(4,1)S(1)}, pred[128]{0:T(512)(128)(4,1)}, u32[]{:S(2)}) copy-start(pred[128]{0:T(512)(128)(4,1)} %copy-done.15) | copy-start | bytes 388
  154.9 35.3 %copy-start.3 = (f32[512,2,32]{2,1,0:T(2,128)}, f32[512,2,32]{2,1,0:T(2,128)S(1)}, u32[]{:S(2)}) copy-start(f32[512,2,32]{2,1,0:T(2,128)S(1)} %scatter_fusion.5) | copy-start | bytes 393220
  161.5 28.7 %copy-start.4 = (f32[512,2,32]{2,1,0:T(2,128)}, f32[512,2,32]{2,1,0:T(2,128)S(1)}, u32[]{:S(2)}) copy-start(f32[512,2,32]{2,1,0:T(2,128)S(1)} %scatter_fusion.3) | copy-start | bytes 393220
  213.0 0.8 copy-start.6
  213.0 1.3 copy-start.5
  213.0 1.8 copy-start.20
  213.0 4.2 copy-start.7
  213.0 4.2 copy-start.22
  213.0 5.3 %copy-start.14 = (f32[16]{0:T(128)S(1)}, f32[16]{0:T(128)}, u32[]{:S(2)}) copy-start(f32[16]{0:T(128)} %copy-done.13) | copy-start | bytes 196
  213.0 5.3 %copy-start.19 = (f32[32]{0:T(128)S(1)}, f32[32]{0:T(128)}, u32[]{:S(2)}) copy-start(f32[32]{0:T(128)} %copy-done.18) | copy-start | bytes 388
  213.0 30.3 %copy-start.23 = (u32[256]{0:T(256)S(1)}, u32[256]{0:T(256)}, u32[]{:S(2)}) copy-start(u32[256]{0:T(256)} %constant.274) | copy-start | bytes 3076
  213.1 255.2 %reduce-scatter.2.cloned.1.call-start = ((), (), s32[]{:S(2)}) async-start(), calls=%async_computation.2 | async-start | bytes 73728 | tf_op jit(solution)/shard_map/reduce_scatter | solution.py:213
  218.5 214.3 %copy-start.10 = (bf16[16,64]{1,0:T(8,128)(2,1)}, bf16[16,64]{1,0:T(8,128)(2,1)S(1)}, u32[]{:S(2)}) copy-start(bf16[16,64]{1,0:T(8,128)(2,1)S(1)} %fusion.71) | copy-start | bytes 6148
Sparse Core Ops, SparseCore 0:
  46.8 46.4 all-gather.3
  213.2 131.2 all-reduce.7
  433.0 35.2 reduce-scatter.1
where the time goes:
time: 478 us; the launch traced here: 476 us
  other arithmetic  137 us (29%)
  waiting for transfers between devices  135 us (28%)
  blocking collectives  132 us (28%)
  local copies, waits for them, and re-layouts  44.5 us (9%)
  between operations  15.1 us (3%)
  matrix products  11.6 us (2%)
    unnamed x4, waiting for transfers between devices  99.7 us
    all_gather x3, blocking collectives, combined_all(): lax.all_gather(part.astype(kind), axis)  77.3 us
    scatter-add x2, other arithmetic, on_device(): sum_rows.at[picked, level_slot]  43.9 us
    reduce_sum x2, other arithmetic, on_device(): filled = jnp.arange(per_tenant) < jnp.sum(member.astype(jnp.int32))  42.6 us
    reduce_scatter x1, waiting for transfers between devices, on_device(): lax.psum_scatter(projected.astype(jnp.bfloat16), 'tp', scatter_dimension=...  35.4 us
    all_gather x1, blocking collectives, on_device(): lax.all_gather(query_rot, 'tp', axis=1, tiled=True)  30.2 us
    all_gather x1, blocking collectives, on_device(): lax.all_gather(new_keyval, 'tp', axis=1, tiled=True)  24.5 us
    scatter-add x2, other arithmetic, on_device(): total_rows.at[picked, level_slot]  13.4 us
  transfers between devices with their start and end apart: 3, of which 2 were waited for; matrix products, arithmetic and copies ran while one was open for 14% of the time, Pallas kernels for 0%

commit v1 on v0

--- a/solution.py
+++ b/solution.py
@@ -3,6 +3,7 @@
 import jax.numpy as jnp
 from jax import lax
 from jax.sharding import PartitionSpec as P
+from jax.lax import all_to_all, axis_size
 
 HEADS = 32
 KV_HEADS = 4
@@ -140,8 +141,14 @@
         .reshape(req_dev, local_kv * HEAD_DIM)
         .astype(jnp.bfloat16)
     )
+
+    def attach_loops(sheet):
+        mesh_dim = "tp"
+        left_arr = jnp.concatenate([sheet for _ in range(axis_size(mesh_dim))], axis=1)
+        return all_to_all(left_arr, mesh_dim, 1, 1, tiled=True)
+
     query_all, keyval_all = (
-        lax.all_gather(query_rot, "tp", axis=1, tiled=True),
+        attach_loops(query_rot),
         lax.all_gather(new_keyval, "tp", axis=1, tiled=True),
     )
     everyone = lax.all_gather(query_all, "grp", axis=0, tiled=True)

time: 478 us -> 464 us (0.971)
  blocking collectives: 132 us -> 118 us
    all_gather x1 -> x0, blocking collectives: 30.2 us -> none  [on_device(): lax.all_gather(query_rot, 'tp', axis=1, tiled=True)]
    all_to_all x0 -> x1, blocking collectives: none -> 16.6 us  [attach_loops(): return all_to_all(left_arr, mesh_dim, 1, 1, tiled=True)]
  transfers between devices with their start and end apart: 3 -> 3, of which waited for: 2 -> 2; matrix products, arithmetic and copies ran while one was open for 14% -> 15% of each run, Pallas kernels for 0% -> 0%
where the time goes in v1:
time: 464 us; the launch traced here: 462 us
  other arithmetic  138 us (30%)
  waiting for transfers between devices  132 us (28%)
  blocking collectives  118 us (25%)
  local copies, waits for them, and re-layouts  45.8 us (10%)
  between operations  15.1 us (3%)
  matrix products  11.5 us (2%)
    unnamed x4, waiting for transfers between devices  96.7 us
    all_gather x3, blocking collectives, combined_all(): lax.all_gather(part.astype(kind), axis)  77.3 us
    scatter-add x2, other arithmetic, on_device(): sum_rows.at[picked, level_slot]  43.9 us
    reduce_sum x2, other arithmetic, on_device(): filled = jnp.arange(per_tenant) < jnp.sum(member.astype(jnp.int32))  42.8 us
    reduce_scatter x1, waiting for transfers between devices, on_device(): lax.psum_scatter(projected.astype(jnp.bfloat16), 'tp', scatter_dimension=...  35.4 us
    all_gather x1, blocking collectives, on_device(): lax.all_gather(new_keyval, 'tp', axis=1, tiled=True)  24.5 us
    all_to_all x1, blocking collectives, attach_loops(): return all_to_all(left_arr, mesh_dim, 1, 1, tiled=True)  16.6 us
    scatter-add x2, other arithmetic, on_device(): total_rows.at[picked, level_slot]  13.4 us
  transfers between devices with their start and end apart: 3, of which 2 were waited for; matrix products, arithmetic and copies ran while one was open for 15% of the time, Pallas kernels for 0%

profile of v1, /device:TPU:10, one launch (start us, length us, event | category | flops | bytes accessed | tf_op | source)
XLA Modules:
  0.0 461.5 jit_solution(16420659284515333162)
XLA Ops:
  7.3 0.8 compare_select_fusion.3
  8.1 1.3 gather_fusion
  9.4 1.3 gather_fusion.2
  10.7 1.3 gather_fusion.1
  12.1 0.7 convert_element_type.148
  12.8 1.0 fusion.32
  13.8 1.6 fusion.59
  15.4 0.7 add_convert_fusion.2
  16.5 16.6 %all_to_all.9 = bf16[16,8,256]{2,0,1:T(8,128)(2,1)S(1)} all-to-all(bf16[16,8,256]{2,0,1:T(8,128)(2,1)S(1)} %concatenate.28), channel_id=1, replica_groups=mesh['grp'=32,'tp'=8] {'tp'}, dimensions={1} | all-to-all | bytes 131072 | tf_op jit(solution)/shard_map/all_to_all | solution.py:148
  33.1 0.6 copy.119
  33.8 0.9 slice_bitcast_fusion.2
  35.0 0.7 copy.79
  35.8 1.6 fusion.90
  37.4 2.1 fusion.87
  39.5 2.1 fusion.88
  41.5 2.1 fusion.89
  43.6 41.5 %convert_reduce_fusion = (s32[]{:T(128)}, pred[512]{0:T(512)(128)(4,1)S(1)}, s32[512]{0:T(512)S(1)}) fusion(s32[512]{0:T(512)} %param.24, s32[]{:T(128)S(6)} %add.231, pred[]{:T(512)S(6)} %lt.150, s32[]{:T(128)} %bitcast.67, s32[]{:T(128)} %bitcast.66, s32[]{:T(128)} %bitcast.65, s32[]{:T(128)} %bitcast.64, s32[]{:T(128)} %bitcast.63, s32[]{:T(128)} %bitcast.62, ...), kind=kLoop, calls=%fused_computation.153 | loop fusion | flops 68607 | bytes 4873 | tf_op jit(solution)/shard_map/reduce_sum | solution.py:167
  85.1 1.3 convert_reduce_fusion.1
  86.5 3.8 top_k.17
  90.3 3.8 top_k.24
  94.0 1.3 fusion.86
  95.3 0.6 iota_compare_fusion.1
  96.0 0.6 iota_compare_fusion
  96.7 1.2 broadcast_compare_fusion.1
  98.0 4.3 gather_fusion.3
  102.3 2.0 broadcast_select_fusion.3
  104.2 2.0 copy.77
  106.3 1.3 fusion.91
  107.7 0.9 copy-done.2
  109.0 1.7 gather_fusion.4
  110.7 1.2 broadcast_select_fusion.2
  112.1 0.3 fusion.92
  113.4 1.6 fusion.18
  115.0 1.3 copy.80
  116.3 1.4 broadcast_select_fusion.1
  117.7 2.1 fusion.16
  119.7 1.6 copy.84
  121.3 1.8 broadcast_select_fusion
  123.2 6.8 %scatter_fusion.4 = f32[512,2,32]{2,1,0:T(2,128)S(1)} fusion(f32[512,2,32]{2,1,0:T(2,128)S(1)} %broadcast.256.clone.1, s32[128]{0:T(128)S(1)} %fusion.77, f32[128,32]{1,0:T(8,128)S(1)} %copy.98), kind=kCustom, calls=%fused_computation.9 | custom fusion | flops 4096 | bytes 50176 | tf_op jit(solution)/shard_map/scatter-add | solution.py:188
  130.2 6.6 %scatter_fusion.2 = f32[512,2,32]{2,1,0:T(2,128)S(1)} fusion(f32[512,2,32]{2,1,0:T(2,128)S(1)} %broadcast.256.clone, s32[128]{0:T(128)S(1)} %fusion.77, f32[128,32]{1,0:T(8,128)S(1)} %copy.86), kind=kCustom, calls=%fused_computation.7 | custom fusion | flops 4096 | bytes 50176 | tf_op jit(solution)/shard_map/scatter-add | solution.py:185
  136.8 6.6 %scatter_fusion.5 = f32[512,2,32]{2,1,0:T(2,128)S(1)} fusion(f32[512,2,32]{2,1,0:T(2,128)S(1)} %scatter_fusion.4, s32[128]{0:T(128)S(1)} %fusion.78, f32[128,32]{1,0:T(8,128)S(1)} %copy.99), kind=kCustom, calls=%fused_computation.10 | custom fusion | flops 4096 | bytes 50176 | tf_op jit(solution)/shard_map/scatter-add | solution.py:188
  143.4 6.6 %scatter_fusion.3 = f32[512,2,32]{2,1,0:T(2,128)S(1)} fusion(f32[512,2,32]{2,1,0:T(2,128)S(1)} %scatter_fusion.2, s32[128]{0:T(128)S(1)} %fusion.78, f32[128,32]{1,0:T(8,128)S(1)} %copy.87), kind=kCustom, calls=%fused_computation.8 | custom fusion | flops 4096 | bytes 50176 | tf_op jit(solution)/shard_map/scatter-add | solution.py:185
  150.0 7.5 %broadcast_in_dim.180 = f32[512,2,2048]{2,1,0:T(2,128)} broadcast(f32[]{:T(128)} %constant.85.clone.1), dimensions={} | broadcast | bytes 8388612 | tf_op jit(solution)/shard_map/broadcast_in_dim | solution.py:176
  157.5 21.2 %scatter_fusion = f32[512,2,2048]{2,1,0:T(2,128)} fusion(f32[512,2,2048]{2,1,0:T(2,128)} %broadcast_in_dim.180, s32[128]{0:T(128)S(1)} %fusion.77, f32[128,2048]{1,0:T(8,128)S(1)} %broadcast_select_fusion.1), kind=kCustom, calls=%fused_computation.5 | custom fusion | flops 262144 | bytes 3146752 | tf_op jit(solution)/shard_map/scatter-add | solution.py:182
  178.7 22.7 %scatter_fusion.1 = f32[512,2,2048]{2,1,0:T(2,128)} fusion(f32[512,2,2048]{2,1,0:T(2,128)} %scatter_fusion, s32[128]{0:T(128)S(1)} %fusion.78, f32[128,2048]{1,0:T(8,128)} %broadcast_select_fusion), kind=kCustom, calls=%fused_computation.6 | custom fusion | flops 262144 | bytes 3146752 | tf_op jit(solution)/shard_map/scatter-add | solution.py:182
  201.5 1.1 copy-done.5
  202.8 0.4 reshape.491
  203.2 1.4 reshape.492
  204.6 1.2 fusion.57
  206.0 24.5 %all-gather.1 = bf16[8,64,16]{1,2,0:T(8,128)(2,1)S(1)} all-gather(bf16[1,64,16]{1,2,0:T(8,128)(2,1)S(1)} %bitcast.287), channel_id=1, replica_groups=mesh['grp'=32,'tp'=8] {'tp'}, dimensions={0}, use_global_device_ids=true | all-gather | bytes 18432 | tf_op jit(solution)/shard_map/all_gather | solution.py:152
  230.8 0.6 dynamic-slice
  232.2 0.8 fusion.93
  233.3 96.6 %all-reduce.8.cloned.1.call-done = (f32[512,2,2048]{2,1,0:T(2,128)}, f32[512,2,32]{2,1,0:T(2,128)}, f32[512,2,32]{2,1,0:T(2,128)}) async-done(((f32[512,2,2048]{2,1,0:T(2,128)}, f32[512,2,32]{2,1,0:T(2,128)}, f32[512,2,32]{2,1,0:T(2,128)}), (f32[512,2,2048]{2,1,0:T(2,128)}, f32[512,2,32]{2,1,0:T(2,128)}, f32[512,2,32]{2,1,0:T(2,128)})) %all-reduce.8.cloned.1.call-update) | async-done | bytes 8650768
  329.9 0.7 constant_dynamic-slice_fusion.3
  331.2 0.7 constant_dynamic-slice_fusion.2
  332.0 26.0 %all_gather.24 = bf16[8,16,4,8]{1,3,2,0:T(8,128)(2,1)S(1)} all-gather(bf16[1,16,4,8]{1,3,2,0:T(8,128)(2,1)S(1)} %fusion.49), channel_id=1, replica_groups=mesh['grp'=32,'tp'=8] {'tp'}, dimensions={0}, use_global_device_ids=true | all-gather | bytes 9216 | tf_op jit(solution)/shard_map/all_gather | solution.py:16
  358.4 1.0 constant_dynamic-slice_fusion.4
  359.8 1.7 fusion.9
  361.5 26.8 %all-gather = bf16[128,4,8,64]{3,2,1,0:T(8,128)(2,1)S(1)} all-gather(bf16[16,4,8,64]{3,2,1,0:T(8,128)(2,1)S(1)} %fusion.9), channel_id=2, replica_groups=mesh['grp'=32,'tp'=8] {'tp'}, dimensions={0}, use_global_device_ids=true | all-gather | bytes 589824 | tf_op jit(solution)/shard_map/all_gather | solution.py:16
  388.3 24.6 %all_gather.23 = bf16[8,16,4,8]{1,3,2,0:T(8,128)(2,1)S(1)} all-gather(bf16[1,16,4,8]{1,3,2,0:T(8,128)(2,1)S(1)} %fusion.56), channel_id=1, replica_groups=mesh['grp'=32,'tp'=8] {'tp'}, dimensions={0}, use_global_device_ids=true | all-gather | bytes 9216 | tf_op jit(solution)/shard_map/all_gather | solution.py:16
  413.0 3.9 while.19
  417.4 0.9 convolution_convert_fusion
  418.3 35.4 %reduce-scatter.2.cloned.1.call-done = bf16[16,256]{1,0:T(8,128)(2,1)} async-done(((bf16[16,2048]{1,0:T(8,128)(2,1)}), bf16[16,256]{1,0:T(8,128)(2,1)}) %reduce-scatter.2.cloned.1.call-update) | async-done | bytes 8208 | tf_op jit(solution)/shard_map/reduce_scatter | solution.py:220
  453.7 1.3 add_convert_fusion.1
  (158 shorter events, 9.8 us)
Async XLA Ops:
  7.2 410.3 %copy-start = (bf16[256,2048]{1,0:T(8,128)(2,1)S(1)}, bf16[256,2048]{1,0:T(8,128)(2,1)}, u32[]{:S(2)}) copy-start(bf16[256,2048]{1,0:T(8,128)(2,1)} %param.19) | copy-start | bytes 3145732
  7.2 90.8 %all-gather.4.cloned.1.call-start = ((), (), s32[]{:S(2)}) async-start(), calls=%async_computation.2 | async-start | bytes 2162688 | tf_op jit(solution)/shard_map/all_gather | solution.py:154
  7.2 27.5 %copy-start.16 = (f32[32]{0:T(128)}, f32[32]{0:T(128)S(1)}, u32[]{:S(2)}) copy-start(f32[32]{0:T(128)S(1)} %multiply_exponential_fusion) | copy-start | bytes 388
  13.7 1.6 copy-start.19
  16.1 18.7 %copy-start.12 = (f32[16]{0:T(128)}, f32[16]{0:T(128)S(1)}, u32[]{:S(2)}) copy-start(f32[16]{0:T(128)S(1)} %add_convert_fusion.2) | copy-start | bytes 196
  33.8 296.1 %all-reduce.8.cloned.1.call-start = ((), (), s32[]{:S(2)}) async-start(), calls=%async_computation.4 | async-start | bytes 18874368
  96.0 16.5 %copy-start.15 = (pred[128]{0:T(512)(128)(4,1)}, pred[128]{0:T(512)(128)(4,1)S(1)}, u32[]{:S(2)}) copy-start(pred[128]{0:T(512)(128)(4,1)S(1)} %iota_compare_fusion.1) | copy-start | bytes 388
  96.6 16.1 %copy-start.14 = (pred[128]{0:T(512)(128)(4,1)}, pred[128]{0:T(512)(128)(4,1)S(1)}, u32[]{:S(2)}) copy-start(pred[128]{0:T(512)(128)(4,1)S(1)} %iota_compare_fusion) | copy-start | bytes 388
  97.9 9.8 %copy-start.11 = (pred[64]{0:T(512)(128)(4,1)}, pred[64]{0:T(512)(128)(4,1)S(1)}, u32[]{:S(2)}) copy-start(pred[64]{0:T(512)(128)(4,1)S(1)} %get-tuple-element.351) | copy-start | bytes 196
  97.9 14.6 %copy-start.10 = (pred[64]{0:T(512)(128)(4,1)}, pred[64]{0:T(512)(128)(4,1)S(1)}, u32[]{:S(2)}) copy-start(pred[64]{0:T(512)(128)(4,1)S(1)} %get-tuple-element.350) | copy-start | bytes 196
  98.0 11.0 %copy-start.1 = (bf16[512,2048]{1,0:T(8,128)(2,1)S(1)}, bf16[512,2048]{1,0:T(8,128)(2,1)}, u32[]{:S(2)}) copy-start(bf16[512,2048]{1,0:T(8,128)(2,1)} %all-gather.4.cloned.1.call-done) | copy-start | bytes 6291460
  107.6 1.0 copy-start.2
  107.6 1.2 copy-start.7
  112.5 0.6 copy-start.8
  143.4 35.3 %copy-start.3 = (f32[512,2,32]{2,1,0:T(2,128)}, f32[512,2,32]{2,1,0:T(2,128)S(1)}, u32[]{:S(2)}) copy-start(f32[512,2,32]{2,1,0:T(2,128)S(1)} %scatter_fusion.5) | copy-start | bytes 393220
  150.0 28.7 %copy-start.4 = (f32[512,2,32]{2,1,0:T(2,128)}, f32[512,2,32]{2,1,0:T(2,128)S(1)}, u32[]{:S(2)}) copy-start(f32[512,2,32]{2,1,0:T(2,128)S(1)} %scatter_fusion.3) | copy-start | bytes 393220
  201.4 1.2 copy-start.5
  201.4 3.2 copy-start.6
  201.4 3.2 copy-start.20
  201.4 4.4 copy-start.13
  201.4 4.4 copy-start.17
  201.4 29.3 %copy-start.21 = (u32[256]{0:T(256)S(1)}, u32[256]{0:T(256)}, u32[]{:S(2)}) copy-start(u32[256]{0:T(256)} %constant.274) | copy-start | bytes 3076
  201.4 30.6 %copy-start.18 = (s32[16]{0:T(128)S(1)}, s32[16]{0:T(128)}, u32[]{:S(2)}) copy-start(s32[16]{0:T(128)} %param.25) | copy-start | bytes 196
  201.5 252.2 %reduce-scatter.2.cloned.1.call-start = ((), (), s32[]{:S(2)}) async-start(), calls=%async_computation.3 | async-start | bytes 73728 | tf_op jit(solution)/shard_map/reduce_scatter | solution.py:220
  206.0 207.0 %copy-start.9 = (bf16[16,64]{1,0:T(8,128)(2,1)}, bf16[16,64]{1,0:T(8,128)(2,1)S(1)}, u32[]{:S(2)}) copy-start(bf16[16,64]{1,0:T(8,128)(2,1)S(1)} %fusion.71) | copy-start | bytes 6148
Sparse Core Ops, SparseCore 0:
  33.9 43.4 all-gather.3
  201.6 128.2 all-reduce.7
  418.5 35.2 reduce-scatter.1
